TPU v7x, 256 devices: a whole 4x4x8 slice. The times are simulated.
256 devices in a mesh: pipe: 8 (over y, x_lo), dp: 32 (over x_hi, z, core).
Axes of the slice: x: 4 (x_hi: 2, x_lo: 2; x = x_hi * 2 + x_lo), y: 4, z: 8, core: 2. Of those that a mesh axis runs over, the one named last changes fastest.
Arguments:
- acts: bfloat16 [8, 8192, 3072], P('pipe', 'dp'), may hold values from -24 to 24, as said below
- grad: float32 [24576, 4096], P('pipe', 'dp'), may hold values from -6 to 6
- owner_of: int32 [8, 12], replicated, may hold values from 0 to 7, as said below
Outputs:
- precond: float32 [24576, 4096], P('pipe', 'dp')
- held_inverse: float32 [8, 24, 256, 256], P('pipe', None, 'dp')
Inputs may be any that keep to these rules, and one draw needn't show every extreme that they name: `acts`: column and token scales of the activations vary; entries lie within the range. `owner_of`: no section index owns more than 24 blocks in all, and some section index owns exactly 24.
All inputs are finite; a program needn't handle non-finite values.
Results may differ from a plain program's by a relative error of at most 0.0003.
Values sent between devices are 32-bit elements; how exact they have to be, the bound alone decides.
No kernel may reach another device: no remote copies, remote signals or barrier semaphores. Data moves between devices by JAX's collectives and lax.ppermute only.
A program may use at most 64 MiB of HBM per device.

v0:
```python
import jax
import jax.numpy as jnp
from jax import lax
from jax.sharding import Mesh
from jax.sharding import PartitionSpec as P

BLK = 256
HOST = 24
DP = ("dp_0", "dp_1", "dp_2")
damping_ratio = 0.1


def in_blocks(value, dim, count):
    before, after = (value.shape[:dim], value.shape[dim + 1 :])
    return jnp.moveaxis(value.reshape(*before, count, -1, *after), dim, 0)


def summed_on_arrival(value, axis, dim):
    count = lax.axis_size(axis)
    tiles = lax.all_to_all(in_blocks(value, dim, count), axis, 0, 0, tiled=True)
    return jnp.sum(tiles, axis=0)


def from_everyone(value, axis):
    count = lax.axis_size(axis)
    return lax.all_to_all(
        jnp.broadcast_to(value[None], (count, *value.shape)), axis, 0, 0, tiled=True
    )


def in_order(tiles, dim):
    lengths = list(tiles.shape[1:])
    lengths[dim] *= tiles.shape[0]
    return jnp.moveaxis(tiles, 0, dim).reshape(lengths)


def collect(value, axis, dim):
    tiles = from_everyone(value, axis)
    return in_order(tiles, dim)


def turned_blocks(tiles, axes, sequence):
    inside = tiles.shape[1:]
    result = tiles.reshape(*(lax.axis_size(a) for a in axes), *inside)
    for k in sequence:
        result = lax.all_to_all(result, axes[k], k, k, tiled=True)
    return result.reshape(-1, *inside)


def exchange_by_chip(value, groups, sequence, split_dim, concat_dim):
    count = lax.axis_size(groups[0]) * lax.axis_size(groups[1])
    tiles = in_blocks(value, split_dim, count)
    return in_order(turned_blocks(tiles, groups, sequence), concat_dim)


def gather_in_order(value, axes, sequence):
    tiles = value[None]
    for k in sequence:
        tiles = lax.all_gather(tiles, axes[k], axis=0, tiled=True)
    carried = [lax.axis_size(axes[k]) for k in reversed(sequence)]
    tiles = tiles.reshape(*carried, *value.shape)
    turned = sorted(range(len(sequence)), key=lambda place: sequence[len(sequence) - 1 - place])
    return tiles.transpose(*turned, *range(len(sequence), tiles.ndim)).reshape(-1, *value.shape)


def gather_axes(value, axes, sequence, dim):
    return in_order(gather_in_order(value, axes, sequence), dim)


def invert_blocks(factor, vacant):
    order_size = factor.shape[-1]
    diagonal_sum = jnp.sum(jnp.diagonal(factor, axis1=1, axis2=2), axis=1)
    damping = damping_ratio * diagonal_sum / order_size
    identity = jnp.eye(order_size, dtype=factor.dtype)
    shifted = factor + (damping + vacant)[:, None, None] * identity
    cholesky_lower = jnp.linalg.cholesky(shifted)
    identity_stack = jnp.broadcast_to(identity, factor.shape)
    inv_lower = lax.linalg.triangular_solve(
        cholesky_lower, identity_stack, left_side=True, lower=True
    )
    return jnp.einsum("mkr,mkc->mrc", inv_lower, inv_lower, precision=lax.Precision.HIGHEST)


def slot_tables(owner_of):
    owners_flat = owner_of.reshape(-1)
    positions = jnp.arange(owners_flat.shape[0], dtype=jnp.int32)
    matches = owners_flat[:, None] == owners_flat[None, :]
    before = positions[None, :] < positions[:, None]
    slot_rank = jnp.sum((matches & before).astype(jnp.int32), axis=1)
    return (owners_flat, slot_rank)


def shards(acts, grad, owner_of):
    tokens = acts.shape[1]
    feature_count = acts.shape[2]
    nblocks = feature_count // BLK
    data_count = lax.axis_size(DP)
    section_count = lax.axis_size("pipe")
    row_share = BLK // data_count
    all_tokens = tokens * data_count
    section_index = lax.axis_index("pipe")
    member = lax.axis_index(DP)
    features = acts[0].reshape(tokens, nblocks, BLK)
    owners_flat, slot_rank = slot_tables(owner_of)
    slot_ids = jnp.arange(HOST, dtype=jnp.int32)
    pick_mine = (
        (owners_flat[None, :] == section_index) & (slot_rank[None, :] == slot_ids[:, None])
    ).astype(jnp.float32)
    own_owners = lax.dynamic_index_in_dim(owner_of, section_index, 0, keepdims=False)
    own_ranks = lax.dynamic_index_in_dim(
        slot_rank.reshape(section_count, nblocks), section_index, 0, keepdims=False
    )
    target = own_owners * HOST + own_ranks
    pick_back = (
        jnp.arange(section_count * HOST, dtype=jnp.int32)[None, :] == target[:, None]
    ).astype(jnp.float32)
    block_terms = jnp.einsum("tbr,tbc->rbc", features, features, preferred_element_type=jnp.float32)
    my_rows = summed_on_arrival(
        block_terms.reshape(row_share * lax.axis_size(DP), nblocks * BLK), DP, 0
    )
    pieces = collect(my_rows, "pipe", 0).reshape(section_count, row_share, nblocks, BLK)
    hosted = jnp.einsum(
        "jsb,srbc->jrc",
        pick_mine.reshape(HOST, section_count, nblocks),
        pieces,
        precision=lax.Precision.HIGHEST,
    )
    occupied = jnp.sum(pick_mine, axis=1)
    per_member = (HOST + data_count - 1) // data_count
    padded_count = per_member * data_count
    padded = jnp.pad(hosted, ((0, padded_count - HOST), (0, 0), (0, 0)))
    mine_blocks = lax.all_to_all(padded, DP, split_axis=0, concat_axis=1, tiled=True) / all_tokens
    padded_flags = jnp.pad(occupied, (0, padded_count - HOST))
    held_flags = lax.dynamic_slice_in_dim(padded_flags, member * per_member, per_member, 0)
    inverted = invert_blocks(mine_blocks, 1.0 - held_flags) * held_flags[:, None, None]
    spread_rows = exchange_by_chip(inverted, (("dp_0", "dp_1"), "dp_2"), (1, 0), 1, 0)
    held_rows = spread_rows[:HOST]
    returned = collect(held_rows, "pipe", 0)
    own_rows = jnp.einsum("bm,mrc->brc", pick_back, returned, precision=lax.Precision.HIGHEST)
    inverse = gather_axes(own_rows, DP, (0, 1, 2), 1)
    grad_blocks = grad.reshape(nblocks, BLK, grad.shape[1])
    precond = jnp.einsum("brk,bkc->brc", inverse, grad_blocks, precision=lax.Precision.HIGHEST)
    return (precond.reshape(feature_count, grad.shape[1]), held_rows[None])


def solution(mesh):
    torus = Mesh(
        mesh.devices.reshape(mesh.shape["pipe"], 2, 8, 2), ("pipe", "dp_0", "dp_1", "dp_2")
    )
    placed = (P("pipe", DP, None), P("pipe", DP), P())
    return jax.shard_map(
        shards,
        mesh=torus,
        in_specs=placed,
        out_specs=(P("pipe", DP), P("pipe", None, DP, None)),
        check_vma=False,
    )
```

profile of v0, /device:TPU:1, one launch (start us, length us, event | category | flops | bytes accessed | tf_op | source)
XLA Modules:
  0.0 336.6 jit_solution(11809143810914962391)
XLA Ops:
  7.2 0.0 copy-start
  7.2 1.8 copy.50
  9.0 2.3 convolution_bitcast_fusion
  11.3 5.2 %copy.52 = f32[256,12,256]{2,1,0:T(8,128)} copy(f32[256,12,256]{0,2,1:T(8,128)} %convolution_bitcast_fusion) | data formatting | bytes 6291456 | tf_op jit(solution)/shard_map/tbr,tbc->rbc/transpose | solution.py:117
  16.5 4.9 %reshape_reshape.7 = f32[32,8,3072]{2,1,0:T(8,128)} reshape(f32[256,12,256]{2,1,0:T(8,128)} %copy.52) | data formatting | bytes 6291456 | tf_op jit(solution)/shard_map/reshape;reshape | solution.py:15
  21.4 85.4 %all_to_all.34 = f32[32,8,3072]{2,1,0:T(8,128)} all-to-all(f32[32,8,3072]{2,1,0:T(8,128)} %reshape_reshape.7), channel_id=1, replica_groups=mesh['pipe'=8,'dp_0'=2,'dp_1'=8,'dp_2'=2] {'dp_0','dp_1','dp_2'}, dimensions={0} | all-to-all | bytes 6291456 | tf_op jit(solution)/shard_map/all_to_all | solution.py:20
  106.7 2.0 reduce_sum.37
  108.8 0.9 broadcast_in_dim.16
  109.7 4.2 %all-to-all-start.1 = ((f32[8,8,3072]{2,1,0:T(8,128)}), f32[8,8,3072]{2,1,0:T(8,128)S(1)}, u32[]{:S(2)}, u32[]{:S(2)}) async-start(f32[8,8,3072]{2,1,0:T(8,128)} %broadcast_in_dim.16), calls=%async_computation.1 | async-start | bytes 1572864 | tf_op jit(solution)/shard_map/all_to_all | solution.py:26
  114.0 0.1 eq.87
  114.0 0.2 convert_reduce_fusion
  114.2 0.1 reshape.236
  114.3 10.0 %all-to-all-done.1 = f32[8,8,3072]{2,1,0:T(8,128)S(1)} async-done(((f32[8,8,3072]{2,1,0:T(8,128)}), f32[8,8,3072]{2,1,0:T(8,128)S(1)}, u32[]{:S(2)}, u32[]{:S(2)}) %all-to-all-start.1) | async-done | bytes 786464 | tf_op jit(solution)/shard_map/all_to_all | solution.py:26
  124.3 0.7 convolution_bitcast_fusion.1
  125.0 0.1 copy.72
  125.1 0.7 pad.9.clone
  125.8 9.9 %all-to-all-start.2 = ((f32[32,8,256]{2,1,0:T(8,128)}), f32[32,8,256]{2,1,0:T(8,128)S(1)}, u32[]{:S(2)}, u32[]{:S(2)}) async-start(f32[32,8,256]{2,1,0:T(8,128)} %pad.9.clone), calls=%async_computation.2 | async-start | bytes 524288 | tf_op jit(solution)/shard_map/all_to_all | solution.py:132
  135.7 0.1 convert_reduce_fusion.1
  135.9 0.7 fusion.26
  136.6 12.5 %all-to-all-done.2 = f32[32,8,256]{2,1,0:T(8,128)S(1)} async-done(((f32[32,8,256]{2,1,0:T(8,128)}), f32[32,8,256]{2,1,0:T(8,128)S(1)}, u32[]{:S(2)}, u32[]{:S(2)}) %all-to-all-start.2) | async-done | bytes 262176 | tf_op jit(solution)/shard_map/all_to_all | solution.py:132
  149.2 2.3 gather_fusion
  151.5 0.6 reduce.19
  152.1 0.1 copy.55
  153.5 0.1 copy.56
  153.7 11.7 %custom-call.16 = f32[1,128,128]{2,1,0:T(8,128)S(1)} custom-call(f32[1,128,128]{2,1,0:T(8,128)S(1)} %cholesky.114), custom_call_target="Cholesky" | custom-call | tf_op jit(solution)/shard_map/jit(cholesky)/cholesky | solution.py:76
  165.4 9.8 %custom-call.17 = f32[1,1,128,128]{2,3,1,0:T(8,128)S(1)} custom-call(f32[1,1,128,128]{3,2,1,0:T(8,128)S(1)} %get-tuple-element.39), custom_call_target="InvertDiagBlocksLowerTriangular" | custom-call | tf_op jit(solution)/shard_map/jit(cholesky)/cholesky | solution.py:76
  175.3 0.2 fusion.8
  175.5 0.3 fusion.2
  175.7 11.7 %custom-call.18 = f32[1,128,128]{2,1,0:T(8,128)S(1)} custom-call(f32[1,128,128]{2,1,0:T(8,128)S(1)} %fusion.2), custom_call_target="Cholesky" | custom-call | tf_op jit(solution)/shard_map/jit(cholesky)/cholesky | solution.py:76
  187.5 0.1 copy.59
  187.6 0.1 copy.58
  187.7 0.1 copy.57
  187.8 0.6 compare_reduce_fusion
  189.7 0.1 triangular_solve.68
  189.8 4.0 %while.1 = (s32[]{:T(128)}, f32[1,256,256]{1,2,0:T(8,128)S(1)}, s32[2,2]{1,0:T(2,128)S(1)}, f32[2,1,128,128]{3,2,1,0:T(8,128)S(1)}, s32[]{:T(128)}) while((s32[]{:T(128)}, f32[1,256,256]{1,2,0:T(8,128)S(1)}, s32[2,2]{1,0:T(2,128)S(1)}, f32[2,1,128,128]{3,2,1,0:T(8,128)S(1)}, s32[]{:T(128)}) %tuple.31), condition=%wide.while_cond, body=%wide.while_body.sunk | while | flops 2 | bytes 393325 | solution.py:78
  189.8 0.6 fusion.38
  190.4 1.3 constant_dynamic-slice_fusion.7
  191.7 0.1 copy.76
  191.8 0.6 fusion.38
  192.4 1.3 constant_dynamic-slice_fusion.7
  193.7 0.1 copy.76
  193.9 19.9 %custom-call.19 = f32[1,2,128,128]{2,3,1,0:T(8,128)S(1)} custom-call(f32[1,2,128,128]{3,2,1,0:T(8,128)S(1)} %bitcast.115), custom_call_target="InvertDiagBlocksLowerTriangular" | custom-call | tf_op jit(solution)/shard_map/triangular_solve | solution.py:78
  213.8 0.3 fusion.7
  214.0 0.4 fusion.1
  214.4 0.3 convolution_bitcast_fusion.2
  214.8 1.3 convolution_multiply_fusion
  216.1 5.1 %all_to_all.35 = f32[16,2,1,8,256]{4,3,0,2,1:T(8,128)S(1)} all-to-all(f32[16,2,1,8,256]{4,3,0,2,1:T(8,128)S(1)} %copy.62), channel_id=1, replica_groups=mesh['pipe'=8,'dp_0'=2,'dp_1'=8,'dp_2'=2] {'dp_2'}, dimensions={1} | all-to-all | bytes 524288 | tf_op jit(solution)/shard_map/all_to_all | solution.py:46
  221.2 13.1 %all_to_all.36 = f32[16,2,1,8,256]{4,3,1,2,0:T(8,128)S(1)} all-to-all(f32[16,2,1,8,256]{4,3,1,2,0:T(8,128)S(1)} %copy.63), channel_id=1, replica_groups=mesh['pipe'=8,'dp_0'=2,'dp_1'=8,'dp_2'=2] {'dp_0','dp_1'}, dimensions={0} | all-to-all | bytes 524288 | tf_op jit(solution)/shard_map/all_to_all | solution.py:46
  234.3 0.1 copy.64
  234.3 1.3 broadcast_in_dim.20
  235.6 3.6 %all-to-all-start.5 = ((f32[8,24,8,256]{3,1,2,0:T(8,128)}), f32[8,24,8,256]{3,1,2,0:T(8,128)S(1)}, u32[]{:S(2)}, u32[]{:S(2)}) async-start(f32[8,24,8,256]{3,1,2,0:T(8,128)} %broadcast_in_dim.20), calls=%async_computation.5 | async-start | bytes 3145728 | tf_op jit(solution)/shard_map/all_to_all | solution.py:26
  239.2 0.0 all-gather.4.cloned.1.call-start
  239.3 18.9 %all-to-all-done.5 = f32[8,24,8,256]{3,1,2,0:T(8,128)S(1)} async-done(((f32[8,24,8,256]{3,1,2,0:T(8,128)}), f32[8,24,8,256]{3,1,2,0:T(8,128)S(1)}, u32[]{:S(2)}, u32[]{:S(2)}) %all-to-all-start.5) | async-done | bytes 1572896 | tf_op jit(solution)/shard_map/all_to_all | solution.py:26
  258.2 0.1 copy.65
  258.3 0.6 fusion.17
  258.9 0.1 copy.66
  259.0 5.8 %all-gather = f32[24,8,256]{2,1,0:T(8,128)} all-gather(f32[12,8,256]{2,1,0:T(8,128)S(1)} %copy.66), channel_id=2, replica_groups=mesh['pipe'=8,'dp_0'=2,'dp_1'=8,'dp_2'=2] {'dp_0'}, dimensions={0}, use_global_device_ids=true | all-gather | bytes 294912 | tf_op jit(solution)/shard_map/all_gather | solution.py:59
  264.8 0.0 all-gather.4.cloned.1.call-update
  264.8 0.0 all-gather.6.cloned.1.call-start
  264.8 36.0 %all-gather.4.cloned.1.call-done = f32[16,12,8,256]{3,2,1,0:T(8,128)} async-done(((f32[2,12,8,256]{3,2,1,0:T(8,128)}), f32[16,12,8,256]{3,2,1,0:T(8,128)}) %all-gather.4.cloned.1.call-update) | async-done | bytes 1572880 | tf_op jit(solution)/shard_map/all_gather | solution.py:59
  300.9 0.0 all-gather.6.cloned.1.call-update
  300.9 22.4 %all-gather.6.cloned.1.call-done = f32[32,12,8,256]{3,2,1,0:T(8,128)} async-done(((f32[16,12,8,256]{3,2,1,0:T(8,128)}), f32[32,12,8,256]{3,2,1,0:T(8,128)}) %all-gather.6.cloned.1.call-update) | async-done | bytes 3145744 | tf_op jit(solution)/shard_map/all_gather | solution.py:59
  323.3 2.3 copy.67
  325.6 4.1 %fusion.27 = f32[12,256,128]{2,1,0:T(8,128)} fusion(f32[12,256,256]{2,1,0:T(8,128)S(1)} %bitcast.105, f32[12,256,128]{2,1,0:T(8,128)S(1)} %bitcast.102), kind=kOutput, calls=%fused_computation.70 | convolution fusion | flops 1207959552 | bytes 6291456 | tf_op jit(solution)/shard_map/brk,bkc->brc/dot_general | solution.py:142
  (29 shorter events, 0.4 us)
Async XLA Ops:
  7.2 318.5 %copy-start = (f32[3072,128]{1,0:T(8,128)S(1)}, f32[3072,128]{1,0:T(8,128)}, u32[]{:S(2)}) copy-start(f32[3072,128]{1,0:T(8,128)} %param.4) | copy-start | bytes 4718596
  108.8 5.2 %copy-start.2 = (s32[8,12]{1,0:T(8,128)S(1)}, s32[8,12]{1,0:T(8,128)}, u32[]{:S(2)}) copy-start(s32[8,12]{1,0:T(8,128)} %param.5) | copy-start | bytes 1156
  109.7 14.6 %all-to-all-start.1 = ((f32[8,8,3072]{2,1,0:T(8,128)}), f32[8,8,3072]{2,1,0:T(8,128)S(1)}, u32[]{:S(2)}, u32[]{:S(2)}) async-start(f32[8,8,3072]{2,1,0:T(8,128)} %broadcast_in_dim.16), calls=%async_computation.1 | async-start | bytes 1572864 | tf_op jit(solution)/shard_map/all_to_all | solution.py:26
  125.8 23.3 %all-to-all-start.2 = ((f32[32,8,256]{2,1,0:T(8,128)}), f32[32,8,256]{2,1,0:T(8,128)S(1)}, u32[]{:S(2)}, u32[]{:S(2)}) async-start(f32[32,8,256]{2,1,0:T(8,128)} %pad.9.clone), calls=%async_computation.2 | async-start | bytes 524288 | tf_op jit(solution)/shard_map/all_to_all | solution.py:132
  234.2 1.4 copy-start.1
  235.6 22.5 %all-to-all-start.5 = ((f32[8,24,8,256]{3,1,2,0:T(8,128)}), f32[8,24,8,256]{3,1,2,0:T(8,128)S(1)}, u32[]{:S(2)}, u32[]{:S(2)}) async-start(f32[8,24,8,256]{3,1,2,0:T(8,128)} %broadcast_in_dim.20), calls=%async_computation.5 | async-start | bytes 3145728 | tf_op jit(solution)/shard_map/all_to_all | solution.py:26
  239.2 61.7 %all-gather.4.cloned.1.call-start = ((), (), s32[]{:S(2)}) async-start(), calls=%async_computation.6 | async-start | bytes 1769472 | tf_op jit(solution)/shard_map/all_gather | solution.py:59
  264.8 58.6 %all-gather.6.cloned.1.call-start = ((), (), s32[]{:S(2)}) async-start(), calls=%async_computation.7 | async-start | bytes 4718592 | tf_op jit(solution)/shard_map/all_gather | solution.py:59
Sparse Core Ops, SparseCore 0:
  264.9 35.9 all-gather.3
  302.7 20.6 all-gather.5
where the time goes:
time: 337 us
  blocking collectives  109 us (32%)
  waiting for transfers between devices  100 us (30%)
  other arithmetic  57.6 us (17%)
  local copies, waits for them, and re-layouts  24.6 us (7%)
  starting transfers between devices  17.8 us (5%)
  between operations  16.8 us (5%)
  matrix products  10.4 us (3%)
    all_to_all x1, blocking collectives, summed_on_arrival(): tiles = lax.all_to_all(in_blocks(value, dim, count), axis, 0, 0, tiled=True)  85.4 us
    all_gather x2, waiting for transfers between devices, gather_in_order(): tiles = lax.all_gather(tiles, axes[k], axis=0, tiled=True)  58.5 us
    another operation x6, other arithmetic, invert_blocks(): cholesky_lower = jnp.linalg.cholesky(shifted)  33.9 us
    all_to_all x2, waiting for transfers between devices, from_everyone(): lax.all_to_all(jnp.broadcast_to(value[None], (count, *value.shape)), axis...  28.9 us
    another operation x3, other arithmetic, invert_blocks(): lax.linalg.triangular_solve(cholesky_lower, identity_stack, left_side=Tru...  19.9 us
    all_to_all x2, blocking collectives, turned_blocks(): result = lax.all_to_all(result, axes[k], k, k, tiled=True)  18.1 us
    all_to_all x1, waiting for transfers between devices, shards(): lax.all_to_all(padded, DP, split_axis=0, concat_axis=1, tiled=True)  12.5 us
    all_to_all x1, starting transfers between devices, shards(): lax.all_to_all(padded, DP, split_axis=0, concat_axis=1, tiled=True)  9.87 us
  transfers between devices with their start and end apart: 5, of which 5 were waited for; matrix products, arithmetic and copies ran while one was open for 0% of the time, Pallas kernels for 0%

commit v1 on v0

--- a/solution.py
+++ b/solution.py
@@ -56,7 +56,8 @@
 def gather_in_order(value, axes, sequence):
     tiles = value[None]
     for k in sequence:
-        tiles = lax.all_gather(tiles, axes[k], axis=0, tiled=True)
+        outgoing = jnp.stack([tiles] * lax.axis_size(axes[k]))
+        tiles = jnp.concatenate(lax.all_to_all(outgoing, axes[k], 0, 0), axis=0)
     carried = [lax.axis_size(axes[k]) for k in reversed(sequence)]
     tiles = tiles.reshape(*carried, *value.shape)
     turned = sorted(range(len(sequence)), key=lambda place: sequence[len(sequence) - 1 - place])

time: 337 us -> 319 us (0.947)
  waiting for transfers between devices: 100 us -> 41.5 us
  blocking collectives: 109 us -> 164 us
  between operations: 16.8 us -> 3.43 us
    all_to_all x0 -> x3, blocking collectives: none -> 60.2 us  [gather_in_order(): tiles = jnp.concatenate(lax.all_to_all(outgoing, axes[k], 0, 0), axis=0)]
    all_gather x2 -> x0, waiting for transfers between devices: 58.5 us -> none  [gather_in_order(): tiles = lax.all_gather(tiles, axes[k], axis=0, tiled=True)]
    all_gather x1 -> x0, blocking collectives: 5.75 us -> none  [gather_in_order(): tiles = lax.all_gather(tiles, axes[k], axis=0, tiled=True)]
  transfers between devices with their start and end apart: 5 -> 3, of which waited for: 5 -> 3; matrix products, arithmetic and copies ran while one was open for 0% -> 0% of each run, Pallas kernels for 0% -> 0%
where the time goes in v1:
time: 319 us; the launch traced here: 318 us
  blocking collectives  164 us (51%)
  other arithmetic  58.1 us (18%)
  waiting for transfers between devices  41.5 us (13%)
  local copies, waits for them, and re-layouts  22.9 us (7%)
  starting transfers between devices  17.7 us (6%)
  matrix products  10.4 us (3%)
  between operations  3.43 us (1%)
    all_to_all x1, blocking collectives, summed_on_arrival(): tiles = lax.all_to_all(in_blocks(value, dim, count), axis, 0, 0, tiled=True)  85.4 us
    all_to_all x3, blocking collectives, gather_in_order(): tiles = jnp.concatenate(lax.all_to_all(outgoing, axes[k], 0, 0), axis=0)  60.2 us
    another operation x6, other arithmetic, invert_blocks(): cholesky_lower = jnp.linalg.cholesky(shifted)  33.9 us
    all_to_all x2, waiting for transfers between devices, from_everyone(): lax.all_to_all(jnp.broadcast_to(value[None], (count, *value.shape)), axis...  28.9 us
    another operation x3, other arithmetic, invert_blocks(): lax.linalg.triangular_solve(cholesky_lower, identity_stack, left_side=Tru...  19.9 us
    all_to_all x2, blocking collectives, turned_blocks(): result = lax.all_to_all(result, axes[k], k, k, tiled=True)  18.1 us
    all_to_all x1, waiting for transfers between devices, shards(): lax.all_to_all(padded, DP, split_axis=0, concat_axis=1, tiled=True)  12.5 us
    all_to_all x1, starting transfers between devices, shards(): lax.all_to_all(padded, DP, split_axis=0, concat_axis=1, tiled=True)  9.87 us
  transfers between devices with their start and end apart: 3, of which 3 were waited for; matrix products, arithmetic and copies ran while one was open for 0% of the time, Pallas kernels for 0%

profile of v1, /device:TPU:1, one launch (start us, length us, event | category | flops | bytes accessed | tf_op | source)
XLA Modules:
  0.0 317.7 jit_solution(10032586673378998228)
XLA Ops:
  0.6 0.0 copy-start
  0.6 1.8 copy.67
  2.5 2.3 convolution_bitcast_fusion
  4.8 5.2 %copy.69 = f32[256,12,256]{2,1,0:T(8,128)} copy(f32[256,12,256]{0,2,1:T(8,128)} %convolution_bitcast_fusion) | data formatting | bytes 6291456 | tf_op jit(solution)/shard_map/tbr,tbc->rbc/transpose | solution.py:118
  10.0 4.9 %reshape_reshape.10 = f32[32,8,3072]{2,1,0:T(8,128)} reshape(f32[256,12,256]{2,1,0:T(8,128)} %copy.69) | data formatting | bytes 6291456 | tf_op jit(solution)/shard_map/reshape;reshape | solution.py:15
  14.8 85.4 %all_to_all.49 = f32[32,8,3072]{2,1,0:T(8,128)} all-to-all(f32[32,8,3072]{2,1,0:T(8,128)} %reshape_reshape.10), channel_id=1, replica_groups=mesh['pipe'=8,'dp_0'=2,'dp_1'=8,'dp_2'=2] {'dp_0','dp_1','dp_2'}, dimensions={0} | all-to-all | bytes 6291456 | tf_op jit(solution)/shard_map/all_to_all | solution.py:20
  100.2 2.0 reduce_sum.37
  102.2 0.0 copy-start.2
  102.3 0.9 broadcast_in_dim.14
  103.2 4.2 %all-to-all-start.1 = ((f32[8,8,3072]{2,1,0:T(8,128)}), f32[8,8,3072]{2,1,0:T(8,128)S(1)}, u32[]{:S(2)}, u32[]{:S(2)}) async-start(f32[8,8,3072]{2,1,0:T(8,128)} %broadcast_in_dim.14), calls=%async_computation.1 | async-start | bytes 1572864 | tf_op jit(solution)/shard_map/all_to_all | solution.py:26
  107.4 0.1 eq.87
  107.5 0.2 convert_reduce_fusion
  107.7 0.1 reshape.235
  107.8 10.0 %all-to-all-done.1 = f32[8,8,3072]{2,1,0:T(8,128)S(1)} async-done(((f32[8,8,3072]{2,1,0:T(8,128)}), f32[8,8,3072]{2,1,0:T(8,128)S(1)}, u32[]{:S(2)}, u32[]{:S(2)}) %all-to-all-start.1) | async-done | bytes 786464 | tf_op jit(solution)/shard_map/all_to_all | solution.py:26
  117.8 0.7 convolution_bitcast_fusion.1
  118.5 0.1 copy.90
  118.6 0.7 pad.9.clone
  119.3 9.9 %all-to-all-start.2 = ((f32[32,8,256]{2,1,0:T(8,128)}), f32[32,8,256]{2,1,0:T(8,128)S(1)}, u32[]{:S(2)}, u32[]{:S(2)}) async-start(f32[32,8,256]{2,1,0:T(8,128)} %pad.9.clone), calls=%async_computation.2 | async-start | bytes 524288 | tf_op jit(solution)/shard_map/all_to_all | solution.py:133
  129.2 0.1 convert_reduce_fusion.1
  129.3 0.7 fusion.28
  130.0 12.5 %all-to-all-done.2 = f32[32,8,256]{2,1,0:T(8,128)S(1)} async-done(((f32[32,8,256]{2,1,0:T(8,128)}), f32[32,8,256]{2,1,0:T(8,128)S(1)}, u32[]{:S(2)}, u32[]{:S(2)}) %all-to-all-start.2) | async-done | bytes 262176 | tf_op jit(solution)/shard_map/all_to_all | solution.py:133
  142.6 2.3 gather_fusion
  145.0 0.6 reduce.19
  145.6 0.1 copy.72
  147.0 0.1 copy.73
  147.2 11.7 %custom-call.16 = f32[1,128,128]{2,1,0:T(8,128)S(1)} custom-call(f32[1,128,128]{2,1,0:T(8,128)S(1)} %cholesky.114), custom_call_target="Cholesky" | custom-call | tf_op jit(solution)/shard_map/jit(cholesky)/cholesky | solution.py:77
  158.9 9.8 %custom-call.17 = f32[1,1,128,128]{2,3,1,0:T(8,128)S(1)} custom-call(f32[1,1,128,128]{3,2,1,0:T(8,128)S(1)} %get-tuple-element.43), custom_call_target="InvertDiagBlocksLowerTriangular" | custom-call | tf_op jit(solution)/shard_map/jit(cholesky)/cholesky | solution.py:77
  168.7 0.2 fusion.11
  168.9 0.3 fusion.5
  169.2 11.7 %custom-call.18 = f32[1,128,128]{2,1,0:T(8,128)S(1)} custom-call(f32[1,128,128]{2,1,0:T(8,128)S(1)} %fusion.5), custom_call_target="Cholesky" | custom-call | tf_op jit(solution)/shard_map/jit(cholesky)/cholesky | solution.py:77
  181.0 0.1 copy.76
  181.1 0.1 copy.75
  181.2 0.1 copy.74
  181.3 0.6 compare_reduce_fusion
  183.2 0.1 triangular_solve.68
  183.3 4.0 %while.1 = (s32[]{:T(128)}, f32[1,256,256]{1,2,0:T(8,128)S(1)}, s32[2,2]{1,0:T(2,128)S(1)}, f32[2,1,128,128]{3,2,1,0:T(8,128)S(1)}, s32[]{:T(128)}) while((s32[]{:T(128)}, f32[1,256,256]{1,2,0:T(8,128)S(1)}, s32[2,2]{1,0:T(2,128)S(1)}, f32[2,1,128,128]{3,2,1,0:T(8,128)S(1)}, s32[]{:T(128)}) %tuple.32), condition=%wide.while_cond, body=%wide.while_body.sunk | while | flops 2 | bytes 393325 | solution.py:79
  183.3 0.6 fusion.38
  183.9 1.3 constant_dynamic-slice_fusion.7
  185.2 0.1 copy.98
  185.3 0.6 fusion.38
  185.9 1.3 constant_dynamic-slice_fusion.7
  187.2 0.1 copy.98
  187.3 19.9 %custom-call.19 = f32[1,2,128,128]{2,3,1,0:T(8,128)S(1)} custom-call(f32[1,2,128,128]{3,2,1,0:T(8,128)S(1)} %bitcast.119), custom_call_target="InvertDiagBlocksLowerTriangular" | custom-call | tf_op jit(solution)/shard_map/triangular_solve | solution.py:79
  207.2 0.3 fusion.10
  207.5 0.4 fusion.4
  207.9 0.3 convolution_bitcast_fusion.2
  208.2 1.3 convolution_multiply_fusion
  209.5 5.1 %all_to_all.50 = f32[16,2,1,8,256]{4,3,0,2,1:T(8,128)S(1)} all-to-all(f32[16,2,1,8,256]{4,3,0,2,1:T(8,128)S(1)} %copy.79), channel_id=1, replica_groups=mesh['pipe'=8,'dp_0'=2,'dp_1'=8,'dp_2'=2] {'dp_2'}, dimensions={1} | all-to-all | bytes 524288 | tf_op jit(solution)/shard_map/all_to_all | solution.py:46
  214.6 13.1 %all_to_all.51 = f32[16,2,1,8,256]{4,3,1,2,0:T(8,128)S(1)} all-to-all(f32[16,2,1,8,256]{4,3,1,2,0:T(8,128)S(1)} %copy.80), channel_id=1, replica_groups=mesh['pipe'=8,'dp_0'=2,'dp_1'=8,'dp_2'=2] {'dp_0','dp_1'}, dimensions={0} | all-to-all | bytes 524288 | tf_op jit(solution)/shard_map/all_to_all | solution.py:46
  227.7 0.0 copy-start.1
  227.7 0.1 copy.81
  227.8 1.3 broadcast_in_dim.16
  229.1 3.6 %all-to-all-start.5 = ((f32[8,24,8,256]{3,1,2,0:T(8,128)}), f32[8,24,8,256]{3,1,2,0:T(8,128)S(1)}, u32[]{:S(2)}, u32[]{:S(2)}) async-start(f32[8,24,8,256]{3,1,2,0:T(8,128)} %broadcast_in_dim.16), calls=%async_computation.5 | async-start | bytes 3145728 | tf_op jit(solution)/shard_map/all_to_all | solution.py:26
  232.7 18.9 %all-to-all-done.5 = f32[8,24,8,256]{3,1,2,0:T(8,128)S(1)} async-done(((f32[8,24,8,256]{3,1,2,0:T(8,128)}), f32[8,24,8,256]{3,1,2,0:T(8,128)S(1)}, u32[]{:S(2)}, u32[]{:S(2)}) %all-to-all-start.5) | async-done | bytes 1572896 | tf_op jit(solution)/shard_map/all_to_all | solution.py:26
  251.6 0.1 copy.82
  251.8 0.6 convolution_bitcast_fusion.4
  252.4 0.1 copy.83
  252.6 7.6 %all_to_all.52 = f32[2,1,12,8,256]{4,3,2,1,0:T(8,128)S(1)} all-to-all(f32[2,1,12,8,256]{4,3,2,1,0:T(8,128)S(1)} %copy.83), channel_id=1, replica_groups=mesh['pipe'=8,'dp_0'=2,'dp_1'=8,'dp_2'=2] {'dp_0'}, dimensions={0} | all-to-all | bytes 393216 | tf_op jit(solution)/shard_map/all_to_all | solution.py:60
  260.1 0.1 stack.10
  260.3 41.3 %all_to_all.53 = f32[8,2,12,8,256]{4,3,2,1,0:T(8,128)S(1)} all-to-all(f32[8,2,12,8,256]{4,3,2,1,0:T(8,128)S(1)} %stack.10), channel_id=1, replica_groups=mesh['pipe'=8,'dp_0'=2,'dp_1'=8,'dp_2'=2] {'dp_1'}, dimensions={0} | all-to-all | bytes 3145728 | tf_op jit(solution)/shard_map/all_to_all | solution.py:60
  301.6 0.4 pad_maximum_fusion
  302.0 11.3 %all_to_all.54 = f32[2,16,12,8,256]{4,3,2,1,0:T(8,128)S(1)} all-to-all(f32[2,16,12,8,256]{4,3,2,1,0:T(8,128)S(1)} %pad_maximum_fusion), channel_id=1, replica_groups=mesh['pipe'=8,'dp_0'=2,'dp_1'=8,'dp_2'=2] {'dp_2'}, dimensions={0} | all-to-all | bytes 6291456 | tf_op jit(solution)/shard_map/all_to_all | solution.py:60
  313.3 0.3 copy.84
  313.6 4.1 %fusion = f32[12,256,128]{2,1,0:T(8,128)} fusion(f32[12,256,128]{2,1,0:T(8,128)S(1)} %bitcast.105, f32[12,32,8,256]{3,2,0,1:T(8,128)S(1)} %bitcast.109), kind=kOutput, calls=%fused_computation.5 | convolution fusion | flops 1207959552 | bytes 6291456 | tf_op jit(solution)/shard_map/brk,bkc->brc/dot_general | solution.py:143
  (28 shorter events, 0.4 us)
Async XLA Ops:
  0.6 313.0 %copy-start = (f32[3072,128]{1,0:T(8,128)S(1)}, f32[3072,128]{1,0:T(8,128)}, u32[]{:S(2)}) copy-start(f32[3072,128]{1,0:T(8,128)} %param.4) | copy-start | bytes 4718596
  102.2 5.2 %copy-start.2 = (s32[8,12]{1,0:T(8,128)S(1)}, s32[8,12]{1,0:T(8,128)}, u32[]{:S(2)}) copy-start(s32[8,12]{1,0:T(8,128)} %param.5) | copy-start | bytes 1156
  103.2 14.6 %all-to-all-start.1 = ((f32[8,8,3072]{2,1,0:T(8,128)}), f32[8,8,3072]{2,1,0:T(8,128)S(1)}, u32[]{:S(2)}, u32[]{:S(2)}) async-start(f32[8,8,3072]{2,1,0:T(8,128)} %broadcast_in_dim.14), calls=%async_computation.1 | async-start | bytes 1572864 | tf_op jit(solution)/shard_map/all_to_all | solution.py:26
  119.3 23.3 %all-to-all-start.2 = ((f32[32,8,256]{2,1,0:T(8,128)}), f32[32,8,256]{2,1,0:T(8,128)S(1)}, u32[]{:S(2)}, u32[]{:S(2)}) async-start(f32[32,8,256]{2,1,0:T(8,128)} %pad.9.clone), calls=%async_computation.2 | async-start | bytes 524288 | tf_op jit(solution)/shard_map/all_to_all | solution.py:133
  227.7 1.4 copy-start.1
  229.1 22.5 %all-to-all-start.5 = ((f32[8,24,8,256]{3,1,2,0:T(8,128)}), f32[8,24,8,256]{3,1,2,0:T(8,128)S(1)}, u32[]{:S(2)}, u32[]{:S(2)}) async-start(f32[8,24,8,256]{3,1,2,0:T(8,128)} %broadcast_in_dim.16), calls=%async_computation.5 | async-start | bytes 3145728 | tf_op jit(solution)/shard_map/all_to_all | solution.py:26
